TPU v7x, 32 devices: a whole 2x2x4 slice. The times are simulated.
32 devices in a mesh: lon: 8 (over z, x), lat: 4 (over y, core).
Axes of the slice: x: 2, y: 2, z: 4, core: 2. Of those that a mesh axis runs over, the one named last changes fastest.
Arguments:
- field: float32 [2, 128, 512], P(None, 'lat', 'lon'), may hold values from -6 to 6
- gamma: float32 [2, 128, 512], P(None, 'lat', 'lon'), may hold values from 1 to 192
- kappa_zonal: float32 [2, 128, 512], P(None, 'lat', 'lon'), may hold values from 4096 to 49152
- kappa_merid: float32 [2, 128, 512], P(None, 'lat', 'lon'), may hold values from 1024 to 12288
- area: float32 [128, 512], P('lat', 'lon'), may hold values from 0.3 to 3
- sea_mask: int32 [128, 512], P('lat', 'lon'), may hold values from 0 to 1, as said below
- fold_pair: int32 [512], P('lon'), may hold values from 0 to 511, as said below
Outputs:
- covaried: float32 [2, 128, 512], P(None, 'lat', 'lon')
Inputs may be any that keep to these rules, and one draw needn't show every extreme that they name: `sea_mask`: ocean cells are 1 and land cells 0; land comes in rectangles, periodic in longitude. A mirror pairing across the fold: fold_pair[i] + i is the same odd number modulo 512 for every i, so fold_pair[fold_pair[i]] == i and fold_pair[i] != i.
All inputs are finite; a program needn't handle non-finite values.
Results may differ from a plain program's by a relative error of at most 0.00095.
Values sent between devices are 32-bit elements; how exact they have to be, the bound alone decides.
No kernel may reach another device: no remote copies, remote signals or barrier semaphores. Data moves between devices by JAX's collectives and lax.ppermute only.
A program may use at most 64 MiB of HBM per device.

v0:
```python
import jax
import jax.numpy as jnp
from jax import lax
from jax.sharding import PartitionSpec as P


def passed_along(block, axis, distance):
    devices = range(lax.axis_size(axis))
    route = [((i - distance) % len(devices), i) for i in devices]
    return lax.ppermute(block, axis, route)


def passed_along_2(value, axis, by):
    size = lax.axis_size(axis)
    pairs = [(i, i + by) for i in range(size) if 0 <= i + by < size]
    return lax.ppermute(value, axis, pairs)


def slide(values, offset, fill, wrap):
    if wrap:
        return jnp.roll(values, offset, axis=-1)
    edge = jnp.full(values.shape[:-1] + (abs(offset),), fill, values.dtype)
    if offset > 0:
        return jnp.concatenate([edge, values[..., :-offset]], axis=-1)
    return jnp.concatenate([values[..., -offset:], edge], axis=-1)


def reduce_lines(lower, diagonal, upper, source, wrap):
    length = source.shape[-1]
    stride = 1
    while stride < length:
        below_diag = slide(diagonal, stride, 1.0, wrap)
        above_diag = slide(diagonal, -stride, 1.0, wrap)
        factor_low = -lower / below_diag
        factor_up = -upper / above_diag
        new_diagonal = (
            diagonal
            + factor_low * slide(upper, stride, 0.0, wrap)
            + factor_up * slide(lower, -stride, 0.0, wrap)
        )
        source = (
            source
            + factor_low * slide(source, stride, 0.0, wrap)
            + factor_up * slide(source, -stride, 0.0, wrap)
        )
        lower = factor_low * slide(lower, stride, 0.0, wrap)
        upper = factor_up * slide(upper, -stride, 0.0, wrap)
        diagonal = new_diagonal
        stride = stride * 2
    if wrap:
        return source / (diagonal + lower + upper)
    return source / diagonal


def cyclic_solve(faces, source):
    before = jnp.roll(faces, 1, axis=-1)
    diagonal = 1.0 + before + faces
    return reduce_lines(-before, diagonal, -faces, source, True)


def open_solve(faces, source):
    before = jnp.concatenate([jnp.zeros_like(faces[..., :1]), faces[..., :-1]], axis=-1)
    diagonal = 1.0 + before + faces
    upper_band = jnp.concatenate([-faces[..., :-1], jnp.zeros_like(faces[..., :1])], axis=-1)
    return reduce_lines(-before, diagonal, upper_band, source, False)


def to_columns(blocks, lanes):
    levels, height, breadth = blocks.shape
    split = blocks.reshape(levels, height, lanes, breadth // lanes)
    return jnp.transpose(split, (2, 0, 3, 1))


def from_columns(pieces):
    lanes, levels, narrow, height = pieces.shape
    return jnp.transpose(pieces, (1, 3, 0, 2)).reshape(levels, height, lanes * narrow)


def local(field, gamma, kappa_zonal, kappa_merid, area, sea_mask, fold_pair):
    ocean_cells = sea_mask.astype(jnp.float32)
    east_edge = passed_along(ocean_cells[:, :1], "lon", -1)
    north_edge = passed_along_2(ocean_cells[:1, :], "lat", -1)
    east_ocean = jnp.concatenate([ocean_cells[:, 1:], east_edge], axis=1)
    north_ocean = jnp.concatenate([ocean_cells[1:], north_edge], axis=0)
    zonal_faces = kappa_zonal * (ocean_cells * east_ocean)[None]
    merid_faces = kappa_merid * (ocean_cells * north_ocean)[None]
    scaled = gamma * ocean_cells[None]
    lanes = lax.axis_size("lat")
    zonal_lines = lax.all_to_all(zonal_faces, "lon", split_axis=1, concat_axis=2, tiled=True)
    merid_lines = lax.all_to_all(
        to_columns(merid_faces, lanes), "lat", split_axis=0, concat_axis=3, tiled=True
    )[0]

    def zonal_pass(current):
        lines = lax.all_to_all(current, "lon", split_axis=1, concat_axis=2, tiled=True)
        return lax.all_to_all(
            cyclic_solve(zonal_lines, lines), "lon", split_axis=2, concat_axis=1, tiled=True
        )

    def merid_open(current):
        return lax.all_to_all(
            to_columns(current, lanes), "lat", split_axis=0, concat_axis=3, tiled=True
        )[0]

    def merid_close(columns):
        return from_columns(
            lax.all_to_all(columns[None], "lat", split_axis=3, concat_axis=0, tiled=True)
        )

    current = zonal_pass(scaled * field)
    columns = open_solve(merid_lines, merid_open(current))
    current = merid_close(columns)
    is_top = lax.axis_index("lat") == lanes - 1

    def fold_natural(values):
        top_cells = values[:, -1, :]
        whole_row = lax.all_gather(top_cells, "lon", axis=1, tiled=True)
        partner = jnp.take(whole_row, fold_pair, axis=1)
        return values.at[:, -1, :].set(jnp.where(is_top, 0.5 * (top_cells + partner), top_cells))

    current = fold_natural(current)
    current = current / area[None]
    current = fold_natural(current)
    current = merid_close(open_solve(merid_lines, merid_open(current)))
    current = zonal_pass(current)
    return scaled * current


def solution(mesh):
    return jax.shard_map(
        local,
        mesh=mesh,
        in_specs=(
            P(None, "lat", "lon"),
            P(None, "lat", "lon"),
            P(None, "lat", "lon"),
            P(None, "lat", "lon"),
            P("lat", "lon"),
            P("lat", "lon"),
            P("lon"),
        ),
        out_specs=P(None, "lat", "lon"),
        check_vma=False,
    )
```

profile of v0, /device:TPU:0, one launch (start us, length us, event | category | flops | bytes accessed | tf_op | source)
XLA Modules:
  0.0 188.0 jit_solution(8956095462419415965)
XLA Ops:
  0.0 0.7 convert_element_type.3
  0.7 1.4 collective-permute-start.1
  2.1 6.0 %collective-permute-start = (f32[32,1]{1,0:T(8,128)S(1)}, f32[32,1]{1,0:T(8,128)S(1)}, u32[]{:S(2)}, u32[]{:S(2)}) collective-permute-start(f32[32,1]{1,0:T(8,128)S(1)} %bitcast.116), channel_id=1, source_target_pairs={{4,0},{8,4},{12,8},{16,12},{20,16},{24,20},{28,24},{0,28},{5,1},{9... | collective-permute-start | bytes 392 | tf_op jit(solution)/shard_map/ppermute | solution.py:10
  8.3 0.7 copy-done
  9.0 0.7 reshape.122
  9.9 0.6 copy-done.1
  10.7 0.7 reshape.120
  11.4 3.5 %all-to-all-start.4 = ((f32[4,1,1024]{2,1,0:T(1,128)}), f32[4,1,1024]{2,1,0:T(1,128)S(1)}, u32[]{:S(2)}, u32[]{:S(2)}) async-start(f32[4,1,1024]{2,1,0:T(1,128)} %reshape.120), calls=%async_computation.4 | async-start | bytes 32768 | tf_op jit(solution)/shard_map/all_to_all | solution.py:90
  15.0 0.7 reshape.124
  15.7 3.1 %all-to-all-done.4 = f32[4,1,1024]{2,1,0:T(1,128)S(1)} async-done(((f32[4,1,1024]{2,1,0:T(1,128)}), f32[4,1,1024]{2,1,0:T(1,128)S(1)}, u32[]{:S(2)}, u32[]{:S(2)}) %all-to-all-start.4) | async-done | bytes 16416 | tf_op jit(solution)/shard_map/all_to_all | solution.py:90
  18.8 5.4 %all-to-all-start = ((f32[8,1,512]{2,1,0:T(1,128)}), f32[8,1,512]{2,1,0:T(1,128)S(1)}, u32[]{:S(2)}, u32[]{:S(2)}) async-start(f32[8,1,512]{2,1,0:T(1,128)} %reshape.122), calls=%async_computation | async-start | bytes 32768 | tf_op jit(solution)/shard_map/all_to_all | solution.py:95
  24.2 0.6 broadcast.223
  24.8 0.7 reduce.8
  25.8 4.9 %all-to-all-done = f32[8,1,512]{2,1,0:T(1,128)S(1)} async-done(((f32[8,1,512]{2,1,0:T(1,128)}), f32[8,1,512]{2,1,0:T(1,128)S(1)}, u32[]{:S(2)}, u32[]{:S(2)}) %all-to-all-start) | async-done | bytes 16416 | tf_op jit(solution)/shard_map/all_to_all | solution.py:95
  30.8 3.3 %all-to-all-start.1 = ((f32[8,1,512]{2,1,0:T(1,128)}), f32[8,1,512]{2,1,0:T(1,128)S(1)}, u32[]{:S(2)}, u32[]{:S(2)}) async-start(f32[8,1,512]{2,1,0:T(1,128)} %reshape.124), calls=%async_computation.1 | async-start | bytes 32768 | tf_op jit(solution)/shard_map/all_to_all | solution.py:89
  34.1 0.7 reduce.5
  35.2 5.4 %all-to-all-done.1 = f32[8,1,512]{2,1,0:T(1,128)S(1)} async-done(((f32[8,1,512]{2,1,0:T(1,128)}), f32[8,1,512]{2,1,0:T(1,128)S(1)}, u32[]{:S(2)}, u32[]{:S(2)}) %all-to-all-start.1) | async-done | bytes 16416 | tf_op jit(solution)/shard_map/all_to_all | solution.py:89
  40.6 0.7 reduce.4
  42.7 0.1 maximum_multiply_fusion.9
  47.9 0.3 copy.67
  48.2 1.3 reshape.126
  49.5 3.3 %all-to-all-start.2 = ((f32[8,1,512]{2,1,0:T(1,128)}), f32[8,1,512]{2,1,0:T(1,128)S(1)}, u32[]{:S(2)}, u32[]{:S(2)}) async-start(f32[8,1,512]{2,1,0:T(1,128)} %reshape.126), calls=%async_computation.2 | async-start | bytes 32768 | tf_op jit(solution)/shard_map/all_to_all | solution.py:96
  52.9 6.4 %all-to-all-done.2 = f32[8,1,512]{2,1,0:T(1,128)S(1)} async-done(((f32[8,1,512]{2,1,0:T(1,128)}), f32[8,1,512]{2,1,0:T(1,128)S(1)}, u32[]{:S(2)}, u32[]{:S(2)}) %all-to-all-start.2) | async-done | bytes 16416 | tf_op jit(solution)/shard_map/all_to_all | solution.py:96
  59.4 0.7 reduce.6
  60.1 0.8 reshape.127
  60.9 0.2 copy.68
  61.1 0.1 reshape.89
  61.4 0.7 reshape.128
  62.1 3.3 %all-to-all-start.3 = ((f32[4,1,1024]{2,1,0:T(1,128)}), f32[4,1,1024]{2,1,0:T(1,128)S(1)}, u32[]{:S(2)}, u32[]{:S(2)}) async-start(f32[4,1,1024]{2,1,0:T(1,128)} %reshape.128), calls=%async_computation.3 | async-start | bytes 32768 | tf_op jit(solution)/shard_map/all_to_all | solution.py:101
  65.4 3.7 %all-to-all-done.3 = f32[4,1,1024]{2,1,0:T(1,128)S(1)} async-done(((f32[4,1,1024]{2,1,0:T(1,128)}), f32[4,1,1024]{2,1,0:T(1,128)S(1)}, u32[]{:S(2)}, u32[]{:S(2)}) %all-to-all-start.3) | async-done | bytes 16416 | tf_op jit(solution)/shard_map/all_to_all | solution.py:101
  69.2 0.7 reduce.7
  73.2 0.1 copy.75
  73.3 0.8 reshape.130
  74.1 3.3 %all-to-all-start.5 = ((f32[4,1,1024]{2,1,0:T(1,128)}), f32[4,1,1024]{2,1,0:T(1,128)S(1)}, u32[]{:S(2)}, u32[]{:S(2)}) async-start(f32[4,1,1024]{2,1,0:T(1,128)} %reshape.130), calls=%async_computation.5 | async-start | bytes 32768 | tf_op jit(solution)/shard_map/all_to_all | solution.py:107
  77.4 3.8 %all-to-all-done.5 = f32[4,1,1024]{2,1,0:T(1,128)S(1)} async-done(((f32[4,1,1024]{2,1,0:T(1,128)}), f32[4,1,1024]{2,1,0:T(1,128)S(1)}, u32[]{:S(2)}, u32[]{:S(2)}) %all-to-all-start.5) | async-done | bytes 16416 | tf_op jit(solution)/shard_map/all_to_all | solution.py:107
  81.2 0.7 reduce.9
  81.9 0.2 reshape.131
  82.1 0.1 copy.98
  82.2 1.0 copy.77
  83.3 30.8 %all-gather = f32[2,1,512]{0,2,1:T(8,128)S(1)} all-gather(f32[2,1,64]{0,2,1:T(8,128)S(1)} %slice.1420), channel_id=2, replica_groups=mesh['lon'=8,'lat'=4] {'lon'}, dimensions={2}, use_global_device_ids=true | all-gather | bytes 4608 | tf_op jit(solution)/shard_map/all_gather | solution.py:117
  114.1 0.6 gather_fusion
  114.8 0.6 copy-done.5
  115.4 0.3 broadcast_divide_fusion
  115.7 30.7 %all-gather.1 = f32[2,1,512]{0,2,1:T(8,128)S(1)} all-gather(f32[2,1,64]{0,2,1:T(8,128)S(1)} %slice.1421), channel_id=3, replica_groups=mesh['lon'=8,'lat'=4] {'lon'}, dimensions={2}, use_global_device_ids=true | all-gather | bytes 4608 | tf_op jit(solution)/shard_map/all_gather | solution.py:117
  146.5 0.6 gather_fusion.1
  147.2 0.6 copy.88
  147.9 6.2 %all_to_all.168 = f32[4,1,1024]{2,1,0:T(1,128)S(1)} all-to-all(f32[4,1,1024]{2,1,0:T(1,128)S(1)} %reshape.132), channel_id=1, replica_groups=mesh['lon'=8,'lat'=4] {'lat'}, dimensions={0} | all-to-all | bytes 32768 | tf_op jit(solution)/shard_map/all_to_all | solution.py:101
  154.1 0.7 reduce.10
  156.1 0.1 divide_bitcast_fusion
  156.2 0.1 copy.90
  156.3 0.2 reshape.134
  156.5 6.2 %all_to_all.169 = f32[4,1,1024]{2,1,0:T(1,128)S(1)} all-to-all(f32[4,1,1024]{2,1,0:T(1,128)S(1)} %reshape.134), channel_id=1, replica_groups=mesh['lon'=8,'lat'=4] {'lat'}, dimensions={0} | all-to-all | bytes 32768 | tf_op jit(solution)/shard_map/all_to_all | solution.py:107
  162.7 0.7 reduce.11
  163.5 0.2 reshape.135
  163.9 0.1 reshape.136
  164.0 8.9 %all_to_all.170 = f32[8,1,512]{2,1,0:T(1,128)S(1)} all-to-all(f32[8,1,512]{2,1,0:T(1,128)S(1)} %reshape.136), channel_id=1, replica_groups=mesh['lon'=8,'lat'=4] {'lon'}, dimensions={0} | all-to-all | bytes 32768 | tf_op jit(solution)/shard_map/all_to_all | solution.py:95
  172.9 0.7 reduce.12
  175.6 0.3 copy.95
  175.9 0.7 reshape.138
  176.6 8.9 %all_to_all.171 = f32[8,1,512]{2,1,0:T(1,128)S(1)} all-to-all(f32[8,1,512]{2,1,0:T(1,128)S(1)} %reshape.138), channel_id=1, replica_groups=mesh['lon'=8,'lat'=4] {'lon'}, dimensions={0} | all-to-all | bytes 32768 | tf_op jit(solution)/shard_map/all_to_all | solution.py:96
  185.6 0.7 reduce.13
  186.3 0.8 reshape.139
  187.1 0.2 copy.103
  187.4 0.6 multiply_multiply_fusion
  (229 shorter events, 14.3 us)
Async XLA Ops:
  0.7 7.5 %copy-start.6 = (s32[64]{0:T(128)S(1)}, s32[64]{0:T(128)}, u32[]{:S(2)}) copy-start(s32[64]{0:T(128)} %param.19) | copy-start | bytes 772
  0.7 9.2 %collective-permute-start.1 = (f32[1,64]{1,0:T(1,128)S(1)}, f32[1,64]{1,0:T(1,128)S(1)}, u32[]{:S(2)}, u32[]{:S(2)}) collective-permute-start(f32[1,64]{1,0:T(1,128)S(1)} %slice.1367), channel_id=1, source_target_pairs={{1,0},{2,1},{3,2},{5,4},{6,5},{7,6},{9,8},{10,9},{11,10},{13,12},{... | collective-permute-start | bytes 776 | tf_op jit(solution)/shard_map/ppermute | solution.py:16
  2.1 7.7 %collective-permute-start = (f32[32,1]{1,0:T(8,128)S(1)}, f32[32,1]{1,0:T(8,128)S(1)}, u32[]{:S(2)}, u32[]{:S(2)}) collective-permute-start(f32[32,1]{1,0:T(8,128)S(1)} %bitcast.116), channel_id=1, source_target_pairs={{4,0},{8,4},{12,8},{16,12},{20,16},{24,20},{28,24},{0,28},{5,1},{9... | collective-permute-start | bytes 392 | tf_op jit(solution)/shard_map/ppermute | solution.py:10
  8.2 0.8 copy-start
  8.2 0.8 copy-start.2
  9.0 0.8 copy-start.3
  9.8 0.7 copy-start.1
  11.4 3.6 %copy-start.4 = (f32[2,32,64]{2,1,0:T(8,128)S(1)}, f32[2,32,64]{2,1,0:T(8,128)}, u32[]{:S(2)}) copy-start(f32[2,32,64]{2,1,0:T(8,128)} %param.15) | copy-start | bytes 49156
  11.4 7.4 %all-to-all-start.4 = ((f32[4,1,1024]{2,1,0:T(1,128)}), f32[4,1,1024]{2,1,0:T(1,128)S(1)}, u32[]{:S(2)}, u32[]{:S(2)}) async-start(f32[4,1,1024]{2,1,0:T(1,128)} %reshape.120), calls=%async_computation.4 | async-start | bytes 32768 | tf_op jit(solution)/shard_map/all_to_all | solution.py:90
  18.8 12.0 %all-to-all-start = ((f32[8,1,512]{2,1,0:T(1,128)}), f32[8,1,512]{2,1,0:T(1,128)S(1)}, u32[]{:S(2)}, u32[]{:S(2)}) async-start(f32[8,1,512]{2,1,0:T(1,128)} %reshape.122), calls=%async_computation | async-start | bytes 32768 | tf_op jit(solution)/shard_map/all_to_all | solution.py:95
  30.8 9.9 %all-to-all-start.1 = ((f32[8,1,512]{2,1,0:T(1,128)}), f32[8,1,512]{2,1,0:T(1,128)S(1)}, u32[]{:S(2)}, u32[]{:S(2)}) async-start(f32[8,1,512]{2,1,0:T(1,128)} %reshape.124), calls=%async_computation.1 | async-start | bytes 32768 | tf_op jit(solution)/shard_map/all_to_all | solution.py:89
  49.5 9.9 %all-to-all-start.2 = ((f32[8,1,512]{2,1,0:T(1,128)}), f32[8,1,512]{2,1,0:T(1,128)S(1)}, u32[]{:S(2)}, u32[]{:S(2)}) async-start(f32[8,1,512]{2,1,0:T(1,128)} %reshape.126), calls=%async_computation.2 | async-start | bytes 32768 | tf_op jit(solution)/shard_map/all_to_all | solution.py:96
  62.1 7.1 %all-to-all-start.3 = ((f32[4,1,1024]{2,1,0:T(1,128)}), f32[4,1,1024]{2,1,0:T(1,128)S(1)}, u32[]{:S(2)}, u32[]{:S(2)}) async-start(f32[4,1,1024]{2,1,0:T(1,128)} %reshape.128), calls=%async_computation.3 | async-start | bytes 32768 | tf_op jit(solution)/shard_map/all_to_all | solution.py:101
  74.1 7.1 %all-to-all-start.5 = ((f32[4,1,1024]{2,1,0:T(1,128)}), f32[4,1,1024]{2,1,0:T(1,128)S(1)}, u32[]{:S(2)}, u32[]{:S(2)}) async-start(f32[4,1,1024]{2,1,0:T(1,128)} %reshape.130), calls=%async_computation.5 | async-start | bytes 32768 | tf_op jit(solution)/shard_map/all_to_all | solution.py:107
  114.7 0.7 copy-start.5
where the time goes:
time: 189 us; the launch traced here: 188 us
  blocking collectives  91.9 us (49%)
  starting transfers between devices  29.6 us (16%)
  waiting for transfers between devices  27.5 us (15%)
  local copies, waits for them, and re-layouts  24.2 us (13%)
  other arithmetic  14 us (7%)
    all_gather x2, blocking collectives, fold_natural(): whole_row = lax.all_gather(top_cells, 'lon', axis=1, tiled=True)  61.6 us
    unnamed x35, local copies, waits for them, and re-layouts  10.7 us
    all_to_all x1, blocking collectives, zonal_pass(): lax.all_to_all(current, 'lon', split_axis=1, concat_axis=2, tiled=True)  8.94 us
    all_to_all x1, blocking collectives, zonal_pass(): lax.all_to_all(cyclic_solve(zonal_lines, lines), 'lon', split_axis=2, con...  8.94 us
    all_to_all x1, waiting for transfers between devices, zonal_pass(): lax.all_to_all(cyclic_solve(zonal_lines, lines), 'lon', split_axis=2, con...  6.44 us
    all_to_all x1, blocking collectives, merid_open(): lax.all_to_all(to_columns(current, lanes), 'lat', split_axis=0, concat_ax...  6.21 us
    all_to_all x1, blocking collectives, merid_close(): lax.all_to_all(columns[None], 'lat', split_axis=3, concat_axis=0, tiled=T...  6.21 us
    ppermute x1, starting transfers between devices, passed_along(): return lax.ppermute(block, axis, route)  6.03 us
  transfers between devices with their start and end apart: 8, of which 6 were waited for; matrix products, arithmetic and copies ran while one was open for 2% of the time, Pallas kernels for 0%

commit v1 on v0

--- a/solution.py
+++ b/solution.py
@@ -114,7 +114,14 @@
 
     def fold_natural(values):
         top_cells = values[:, -1, :]
-        whole_row = lax.all_gather(top_cells, "lon", axis=1, tiled=True)
+        ring = [top_cells]
+        for hop in range(7):
+            ring.append(lax.ppermute(ring[-1], "lon", [(dev, (dev + 1) % 8) for dev in range(8)]))
+        whole_row = jnp.roll(
+            jnp.concatenate(ring[::-1], axis=1),
+            (lax.axis_index("lon") + 1) * ring[0].shape[1],
+            axis=1,
+        )
         partner = jnp.take(whole_row, fold_pair, axis=1)
         return values.at[:, -1, :].set(jnp.where(is_top, 0.5 * (top_cells + partner), top_cells))
 

time: 189 us -> 212 us (1.12)
  waiting for transfers between devices: 27.5 us -> 111 us
  blocking collectives: 91.9 us -> 36.5 us
  starting transfers between devices: 29.6 us -> 25.9 us
    ppermute x0 -> x14, waiting for transfers between devices: none -> 86.8 us  [fold_natural(): lax.ppermute(ring[-1], 'lon', [(dev, (dev + 1) % 8) for dev in range(8)])]
    all_gather x2 -> x0, blocking collectives: 61.6 us -> none  [fold_natural(): whole_row = lax.all_gather(top_cells, 'lon', axis=1, tiled=True)]
    all_to_all x1 -> x2, blocking collectives: 6.21 us -> 12.4 us  [merid_close(): lax.all_to_all(columns[None], 'lat', split_axis=3, concat_axis=0, tiled=T...]
    all_to_all x1 -> x0, waiting for transfers between devices: 3.8 us -> none  [merid_close(): lax.all_to_all(columns[None], 'lat', split_axis=3, concat_axis=0, tiled=T...]
    all_to_all x1 -> x0, starting transfers between devices: 3.25 us -> none  [merid_close(): lax.all_to_all(columns[None], 'lat', split_axis=3, concat_axis=0, tiled=T...]
    unnamed x35 -> x38, local copies, waits for them, and re-layouts: 10.7 us -> 8.58 us
  transfers between devices with their start and end apart: 8 -> 21, of which waited for: 6 -> 20; matrix products, arithmetic and copies ran while one was open for 2% -> 2% of each run, Pallas kernels for 0% -> 0%
where the time goes in v1:
time: 212 us; the launch traced here: 211 us
  waiting for transfers between devices  111 us (52%)
  blocking collectives  36.5 us (17%)
  starting transfers between devices  25.9 us (12%)
  local copies, waits for them, and re-layouts  22.8 us (11%)
  other arithmetic  13.3 us (6%)
    ppermute x14, waiting for transfers between devices, fold_natural(): lax.ppermute(ring[-1], 'lon', [(dev, (dev + 1) % 8) for dev in range(8)])  86.8 us
    all_to_all x2, blocking collectives, merid_close(): lax.all_to_all(columns[None], 'lat', split_axis=3, concat_axis=0, tiled=T...  12.4 us
    all_to_all x1, blocking collectives, zonal_pass(): lax.all_to_all(cyclic_solve(zonal_lines, lines), 'lon', split_axis=2, con...  8.94 us
    all_to_all x1, blocking collectives, zonal_pass(): lax.all_to_all(current, 'lon', split_axis=1, concat_axis=2, tiled=True)  8.94 us
    unnamed x38, local copies, waits for them, and re-layouts  8.58 us
    all_to_all x1, waiting for transfers between devices, zonal_pass(): lax.all_to_all(cyclic_solve(zonal_lines, lines), 'lon', split_axis=2, con...  6.44 us
    all_to_all x1, blocking collectives, merid_open(): lax.all_to_all(to_columns(current, lanes), 'lat', split_axis=0, concat_ax...  6.21 us
    ppermute x1, starting transfers between devices, passed_along(): return lax.ppermute(block, axis, route)  5.98 us
  transfers between devices with their start and end apart: 21, of which 20 were waited for; matrix products, arithmetic and copies ran while one was open for 2% of the time, Pallas kernels for 0%

profile of v1, /device:TPU:0, one launch (start us, length us, event | category | flops | bytes accessed | tf_op | source)
XLA Modules:
  0.0 210.7 jit_solution(10228915387783692958)
XLA Ops:
  0.0 0.7 convert_element_type.3
  0.7 6.0 %collective-permute-start = (f32[32,1]{1,0:T(8,128)S(1)}, f32[32,1]{1,0:T(8,128)S(1)}, u32[]{:S(2)}, u32[]{:S(2)}) collective-permute-start(f32[32,1]{1,0:T(8,128)S(1)} %bitcast.111), channel_id=1, source_target_pairs={{4,0},{8,4},{12,8},{16,12},{20,16},{24,20},{28,24},{0,28},{5,1},{9... | collective-permute-start | bytes 392 | tf_op jit(solution)/shard_map/ppermute | solution.py:10
  6.7 1.4 collective-permute-start.1
  8.3 0.7 reshape.122
  9.1 0.7 collective-permute-done.1
  10.0 0.7 reshape.120
  10.7 3.5 %all-to-all-start.4 = ((f32[4,1,1024]{2,1,0:T(1,128)}), f32[4,1,1024]{2,1,0:T(1,128)S(1)}, u32[]{:S(2)}, u32[]{:S(2)}) async-start(f32[4,1,1024]{2,1,0:T(1,128)} %reshape.120), calls=%async_computation.4 | async-start | bytes 32768 | tf_op jit(solution)/shard_map/all_to_all | solution.py:90
  14.3 0.7 reshape.124
  15.0 3.1 %all-to-all-done.4 = f32[4,1,1024]{2,1,0:T(1,128)S(1)} async-done(((f32[4,1,1024]{2,1,0:T(1,128)}), f32[4,1,1024]{2,1,0:T(1,128)S(1)}, u32[]{:S(2)}, u32[]{:S(2)}) %all-to-all-start.4) | async-done | bytes 16416 | tf_op jit(solution)/shard_map/all_to_all | solution.py:90
  18.1 4.4 %all-to-all-start = ((f32[8,1,512]{2,1,0:T(1,128)}), f32[8,1,512]{2,1,0:T(1,128)S(1)}, u32[]{:S(2)}, u32[]{:S(2)}) async-start(f32[8,1,512]{2,1,0:T(1,128)} %reshape.122), calls=%async_computation | async-start | bytes 32768 | tf_op jit(solution)/shard_map/all_to_all | solution.py:95
  22.5 0.6 broadcast.226
  23.1 0.7 reduce.12
  24.1 5.0 %all-to-all-done = f32[8,1,512]{2,1,0:T(1,128)S(1)} async-done(((f32[8,1,512]{2,1,0:T(1,128)}), f32[8,1,512]{2,1,0:T(1,128)S(1)}, u32[]{:S(2)}, u32[]{:S(2)}) %all-to-all-start) | async-done | bytes 16416 | tf_op jit(solution)/shard_map/all_to_all | solution.py:95
  29.1 3.3 %all-to-all-start.1 = ((f32[8,1,512]{2,1,0:T(1,128)}), f32[8,1,512]{2,1,0:T(1,128)S(1)}, u32[]{:S(2)}, u32[]{:S(2)}) async-start(f32[8,1,512]{2,1,0:T(1,128)} %reshape.124), calls=%async_computation.1 | async-start | bytes 32768 | tf_op jit(solution)/shard_map/all_to_all | solution.py:89
  32.4 0.7 reduce.9
  33.4 5.5 %all-to-all-done.1 = f32[8,1,512]{2,1,0:T(1,128)S(1)} async-done(((f32[8,1,512]{2,1,0:T(1,128)}), f32[8,1,512]{2,1,0:T(1,128)S(1)}, u32[]{:S(2)}, u32[]{:S(2)}) %all-to-all-start.1) | async-done | bytes 16416 | tf_op jit(solution)/shard_map/all_to_all | solution.py:89
  38.9 0.7 reduce.8
  46.2 0.3 copy.73
  46.4 1.3 reshape.126
  47.8 3.3 %all-to-all-start.2 = ((f32[8,1,512]{2,1,0:T(1,128)}), f32[8,1,512]{2,1,0:T(1,128)S(1)}, u32[]{:S(2)}, u32[]{:S(2)}) async-start(f32[8,1,512]{2,1,0:T(1,128)} %reshape.126), calls=%async_computation.2 | async-start | bytes 32768 | tf_op jit(solution)/shard_map/all_to_all | solution.py:96
  51.2 6.4 %all-to-all-done.2 = f32[8,1,512]{2,1,0:T(1,128)S(1)} async-done(((f32[8,1,512]{2,1,0:T(1,128)}), f32[8,1,512]{2,1,0:T(1,128)S(1)}, u32[]{:S(2)}, u32[]{:S(2)}) %all-to-all-start.2) | async-done | bytes 16416 | tf_op jit(solution)/shard_map/all_to_all | solution.py:96
  57.6 0.7 reduce.10
  58.3 0.8 reshape.127
  59.1 0.2 copy.74
  59.6 0.7 reshape.128
  60.3 3.3 %all-to-all-start.3 = ((f32[4,1,1024]{2,1,0:T(1,128)}), f32[4,1,1024]{2,1,0:T(1,128)S(1)}, u32[]{:S(2)}, u32[]{:S(2)}) async-start(f32[4,1,1024]{2,1,0:T(1,128)} %reshape.128), calls=%async_computation.3 | async-start | bytes 32768 | tf_op jit(solution)/shard_map/all_to_all | solution.py:101
  63.6 3.7 %all-to-all-done.3 = f32[4,1,1024]{2,1,0:T(1,128)S(1)} async-done(((f32[4,1,1024]{2,1,0:T(1,128)}), f32[4,1,1024]{2,1,0:T(1,128)S(1)}, u32[]{:S(2)}, u32[]{:S(2)}) %all-to-all-start.3) | async-done | bytes 16416 | tf_op jit(solution)/shard_map/all_to_all | solution.py:101
  67.4 0.7 reduce.11
  71.6 6.2 %all_to_all.168 = f32[4,1,1024]{2,1,0:T(1,128)S(1)} all-to-all(f32[4,1,1024]{2,1,0:T(1,128)S(1)} %reshape.130), channel_id=1, replica_groups=mesh['lon'=8,'lat'=4] {'lat'}, dimensions={0} | all-to-all | bytes 32768 | tf_op jit(solution)/shard_map/all_to_all | solution.py:107
  77.8 0.7 reduce.13
  78.5 0.2 reshape.131
  79.0 0.6 collective-permute-start.2
  79.6 5.7 %collective-permute-done.2 = f32[2,64]{1,0:T(2,128)S(1)} collective-permute-done((f32[2,64]{1,0:T(2,128)S(1)}, f32[2,64]{1,0:T(2,128)S(1)}, u32[]{:S(2)}, u32[]{:S(2)}) %collective-permute-start.2) | collective-permute-done | bytes 544 | tf_op jit(solution)/shard_map/ppermute | solution.py:119
  85.4 6.3 %collective-permute-done.3 = f32[2,64]{1,0:T(2,128)S(1)} collective-permute-done((f32[2,64]{1,0:T(2,128)S(1)}, f32[2,64]{1,0:T(2,128)S(1)}, u32[]{:S(2)}, u32[]{:S(2)}) %collective-permute-start.3) | collective-permute-done | bytes 544 | tf_op jit(solution)/shard_map/ppermute | solution.py:119
  91.6 6.3 %collective-permute-done.4 = f32[2,64]{1,0:T(2,128)S(1)} collective-permute-done((f32[2,64]{1,0:T(2,128)S(1)}, f32[2,64]{1,0:T(2,128)S(1)}, u32[]{:S(2)}, u32[]{:S(2)}) %collective-permute-start.4) | collective-permute-done | bytes 544 | tf_op jit(solution)/shard_map/ppermute | solution.py:119
  97.9 6.2 %collective-permute-done.5 = f32[2,64]{1,0:T(2,128)S(1)} collective-permute-done((f32[2,64]{1,0:T(2,128)S(1)}, f32[2,64]{1,0:T(2,128)S(1)}, u32[]{:S(2)}, u32[]{:S(2)}) %collective-permute-start.5) | collective-permute-done | bytes 544 | tf_op jit(solution)/shard_map/ppermute | solution.py:119
  104.1 6.3 %collective-permute-done.6 = f32[2,64]{1,0:T(2,128)S(1)} collective-permute-done((f32[2,64]{1,0:T(2,128)S(1)}, f32[2,64]{1,0:T(2,128)S(1)}, u32[]{:S(2)}, u32[]{:S(2)}) %collective-permute-start.6) | collective-permute-done | bytes 544 | tf_op jit(solution)/shard_map/ppermute | solution.py:119
  110.4 6.3 %collective-permute-done.7 = f32[2,64]{1,0:T(2,128)S(1)} collective-permute-done((f32[2,64]{1,0:T(2,128)S(1)}, f32[2,64]{1,0:T(2,128)S(1)}, u32[]{:S(2)}, u32[]{:S(2)}) %collective-permute-start.7) | collective-permute-done | bytes 544 | tf_op jit(solution)/shard_map/ppermute | solution.py:119
  116.9 6.1 %collective-permute-done.8 = f32[2,64]{1,0:T(2,128)S(1)} collective-permute-done((f32[2,64]{1,0:T(2,128)S(1)}, f32[2,64]{1,0:T(2,128)S(1)}, u32[]{:S(2)}, u32[]{:S(2)}) %collective-permute-start.8) | collective-permute-done | bytes 544 | tf_op jit(solution)/shard_map/ppermute | solution.py:119
  123.3 0.6 gather_fusion
  124.0 0.5 copy.88
  124.5 0.3 scatter.6
  125.1 6.3 %collective-permute-done.9 = f32[2,64]{1,0:T(2,128)S(1)} collective-permute-done((f32[2,64]{1,0:T(2,128)S(1)}, f32[2,64]{1,0:T(2,128)S(1)}, u32[]{:S(2)}, u32[]{:S(2)}) %collective-permute-start.9) | collective-permute-done | bytes 544 | tf_op jit(solution)/shard_map/ppermute | solution.py:119
  131.3 6.3 %collective-permute-done.10 = f32[2,64]{1,0:T(2,128)S(1)} collective-permute-done((f32[2,64]{1,0:T(2,128)S(1)}, f32[2,64]{1,0:T(2,128)S(1)}, u32[]{:S(2)}, u32[]{:S(2)}) %collective-permute-start.10) | collective-permute-done | bytes 544 | tf_op jit(solution)/shard_map/ppermute | solution.py:119
  137.6 6.3 %collective-permute-done.11 = f32[2,64]{1,0:T(2,128)S(1)} collective-permute-done((f32[2,64]{1,0:T(2,128)S(1)}, f32[2,64]{1,0:T(2,128)S(1)}, u32[]{:S(2)}, u32[]{:S(2)}) %collective-permute-start.11) | collective-permute-done | bytes 544 | tf_op jit(solution)/shard_map/ppermute | solution.py:119
  143.8 6.3 %collective-permute-done.12 = f32[2,64]{1,0:T(2,128)S(1)} collective-permute-done((f32[2,64]{1,0:T(2,128)S(1)}, f32[2,64]{1,0:T(2,128)S(1)}, u32[]{:S(2)}, u32[]{:S(2)}) %collective-permute-start.12) | collective-permute-done | bytes 544 | tf_op jit(solution)/shard_map/ppermute | solution.py:119
  150.1 6.3 %collective-permute-done.13 = f32[2,64]{1,0:T(2,128)S(1)} collective-permute-done((f32[2,64]{1,0:T(2,128)S(1)}, f32[2,64]{1,0:T(2,128)S(1)}, u32[]{:S(2)}, u32[]{:S(2)}) %collective-permute-start.13) | collective-permute-done | bytes 544 | tf_op jit(solution)/shard_map/ppermute | solution.py:119
  156.4 6.3 %collective-permute-done.14 = f32[2,64]{1,0:T(2,128)S(1)} collective-permute-done((f32[2,64]{1,0:T(2,128)S(1)}, f32[2,64]{1,0:T(2,128)S(1)}, u32[]{:S(2)}, u32[]{:S(2)}) %collective-permute-start.14) | collective-permute-done | bytes 544 | tf_op jit(solution)/shard_map/ppermute | solution.py:119
  162.7 6.2 %collective-permute-done.15 = f32[2,64]{1,0:T(2,128)S(1)} collective-permute-done((f32[2,64]{1,0:T(2,128)S(1)}, f32[2,64]{1,0:T(2,128)S(1)}, u32[]{:S(2)}, u32[]{:S(2)}) %collective-permute-start.15) | collective-permute-done | bytes 544 | tf_op jit(solution)/shard_map/ppermute | solution.py:119
  169.3 0.6 gather_fusion.1
  169.9 0.5 copy.94
  170.5 0.3 scatter.9
  170.9 6.2 %all_to_all.169 = f32[4,1,1024]{2,1,0:T(1,128)S(1)} all-to-all(f32[4,1,1024]{2,1,0:T(1,128)S(1)} %reshape.132), channel_id=1, replica_groups=mesh['lon'=8,'lat'=4] {'lat'}, dimensions={0} | all-to-all | bytes 32768 | tf_op jit(solution)/shard_map/all_to_all | solution.py:101
  177.1 0.7 reduce.14
  179.4 6.2 %all_to_all.170 = f32[4,1,1024]{2,1,0:T(1,128)S(1)} all-to-all(f32[4,1,1024]{2,1,0:T(1,128)S(1)} %reshape.134), channel_id=1, replica_groups=mesh['lon'=8,'lat'=4] {'lat'}, dimensions={0} | all-to-all | bytes 32768 | tf_op jit(solution)/shard_map/all_to_all | solution.py:107
  185.7 0.7 reduce.15
  186.8 8.9 %all_to_all.171 = f32[8,1,512]{2,1,0:T(1,128)S(1)} all-to-all(f32[8,1,512]{2,1,0:T(1,128)S(1)} %reshape.136), channel_id=1, replica_groups=mesh['lon'=8,'lat'=4] {'lon'}, dimensions={0} | all-to-all | bytes 32768 | tf_op jit(solution)/shard_map/all_to_all | solution.py:95
  195.8 0.7 reduce.16
  198.4 0.3 copy.102
  198.7 0.7 reshape.138
  199.4 8.9 %all_to_all.172 = f32[8,1,512]{2,1,0:T(1,128)S(1)} all-to-all(f32[8,1,512]{2,1,0:T(1,128)S(1)} %reshape.138), channel_id=1, replica_groups=mesh['lon'=8,'lat'=4] {'lon'}, dimensions={0} | all-to-all | bytes 32768 | tf_op jit(solution)/shard_map/all_to_all | solution.py:96
  208.4 0.7 reduce.17
  209.0 0.8 reshape.139
  210.1 0.6 multiply_multiply_fusion
  (267 shorter events, 17.3 us)
Async XLA Ops:
  0.7 8.4 %collective-permute-start = (f32[32,1]{1,0:T(8,128)S(1)}, f32[32,1]{1,0:T(8,128)S(1)}, u32[]{:S(2)}, u32[]{:S(2)}) collective-permute-start(f32[32,1]{1,0:T(8,128)S(1)} %bitcast.111), channel_id=1, source_target_pairs={{4,0},{8,4},{12,8},{16,12},{20,16},{24,20},{28,24},{0,28},{5,1},{9... | collective-permute-start | bytes 392 | tf_op jit(solution)/shard_map/ppermute | solution.py:10
  6.7 1.5 copy-start
  6.7 1.5 copy-start.2
  6.7 3.1 %collective-permute-start.1 = (f32[1,64]{1,0:T(1,128)S(1)}, f32[1,64]{1,0:T(1,128)S(1)}, u32[]{:S(2)}, u32[]{:S(2)}) collective-permute-start(f32[1,64]{1,0:T(1,128)S(1)} %slice.1367), channel_id=1, source_target_pairs={{1,0},{2,1},{3,2},{5,4},{6,5},{7,6},{9,8},{10,9},{11,10},{13,12},{... | collective-permute-start | bytes 776 | tf_op jit(solution)/shard_map/ppermute | solution.py:16
  8.3 0.8 copy-start.3
  9.0 0.8 copy-start.1
  10.7 3.6 %copy-start.4 = (f32[2,32,64]{2,1,0:T(8,128)S(1)}, f32[2,32,64]{2,1,0:T(8,128)}, u32[]{:S(2)}) copy-start(f32[2,32,64]{2,1,0:T(8,128)} %param.17) | copy-start | bytes 49156
  10.7 7.4 %all-to-all-start.4 = ((f32[4,1,1024]{2,1,0:T(1,128)}), f32[4,1,1024]{2,1,0:T(1,128)S(1)}, u32[]{:S(2)}, u32[]{:S(2)}) async-start(f32[4,1,1024]{2,1,0:T(1,128)} %reshape.120), calls=%async_computation.4 | async-start | bytes 32768 | tf_op jit(solution)/shard_map/all_to_all | solution.py:90
  18.1 11.0 %all-to-all-start = ((f32[8,1,512]{2,1,0:T(1,128)}), f32[8,1,512]{2,1,0:T(1,128)S(1)}, u32[]{:S(2)}, u32[]{:S(2)}) async-start(f32[8,1,512]{2,1,0:T(1,128)} %reshape.122), calls=%async_computation | async-start | bytes 32768 | tf_op jit(solution)/shard_map/all_to_all | solution.py:95
  29.1 9.9 %all-to-all-start.1 = ((f32[8,1,512]{2,1,0:T(1,128)}), f32[8,1,512]{2,1,0:T(1,128)S(1)}, u32[]{:S(2)}, u32[]{:S(2)}) async-start(f32[8,1,512]{2,1,0:T(1,128)} %reshape.124), calls=%async_computation.1 | async-start | bytes 32768 | tf_op jit(solution)/shard_map/all_to_all | solution.py:89
  47.8 9.9 %all-to-all-start.2 = ((f32[8,1,512]{2,1,0:T(1,128)}), f32[8,1,512]{2,1,0:T(1,128)S(1)}, u32[]{:S(2)}, u32[]{:S(2)}) async-start(f32[8,1,512]{2,1,0:T(1,128)} %reshape.126), calls=%async_computation.2 | async-start | bytes 32768 | tf_op jit(solution)/shard_map/all_to_all | solution.py:96
  60.3 7.1 %all-to-all-start.3 = ((f32[4,1,1024]{2,1,0:T(1,128)}), f32[4,1,1024]{2,1,0:T(1,128)S(1)}, u32[]{:S(2)}, u32[]{:S(2)}) async-start(f32[4,1,1024]{2,1,0:T(1,128)} %reshape.128), calls=%async_computation.3 | async-start | bytes 32768 | tf_op jit(solution)/shard_map/all_to_all | solution.py:101
  78.8 6.5 %copy-start.6 = (s32[64]{0:T(128)S(1)}, s32[64]{0:T(128)}, u32[]{:S(2)}) copy-start(s32[64]{0:T(128)} %param.21) | copy-start | bytes 772
  79.0 6.3 %collective-permute-start.2 = (f32[2,64]{1,0:T(2,128)S(1)}, f32[2,64]{1,0:T(2,128)S(1)}, u32[]{:S(2)}, u32[]{:S(2)}) collective-permute-start(f32[2,64]{1,0:T(2,128)S(1)} %slice_reduce_fusion.1), channel_id=1, source_target_pairs={{0,4},{4,8},{8,12},{12,16},{16,20},{20,24},{24,28},{28,0},{1,5},{5... | collective-permute-start | bytes 1544 | tf_op jit(solution)/shard_map/ppermute | solution.py:119
  85.3 6.3 %collective-permute-start.3 = (f32[2,64]{1,0:T(2,128)S(1)}, f32[2,64]{1,0:T(2,128)S(1)}, u32[]{:S(2)}, u32[]{:S(2)}) collective-permute-start(f32[2,64]{1,0:T(2,128)S(1)} %collective-permute-done.2), channel_id=1, source_target_pairs={{0,4},{4,8},{8,12},{12,16},{16,20},{20,24},{24,28},{28,0},{1,5},{5... | collective-permute-start | bytes 1544 | tf_op jit(solution)/shard_map/ppermute | solution.py:119
  91.6 6.3 %collective-permute-start.4 = (f32[2,64]{1,0:T(2,128)S(1)}, f32[2,64]{1,0:T(2,128)S(1)}, u32[]{:S(2)}, u32[]{:S(2)}) collective-permute-start(f32[2,64]{1,0:T(2,128)S(1)} %collective-permute-done.3), channel_id=1, source_target_pairs={{0,4},{4,8},{8,12},{12,16},{16,20},{20,24},{24,28},{28,0},{1,5},{5... | collective-permute-start | bytes 1544 | tf_op jit(solution)/shard_map/ppermute | solution.py:119
  97.9 6.3 %collective-permute-start.5 = (f32[2,64]{1,0:T(2,128)S(1)}, f32[2,64]{1,0:T(2,128)S(1)}, u32[]{:S(2)}, u32[]{:S(2)}) collective-permute-start(f32[2,64]{1,0:T(2,128)S(1)} %collective-permute-done.4), channel_id=1, source_target_pairs={{0,4},{4,8},{8,12},{12,16},{16,20},{20,24},{24,28},{28,0},{1,5},{5... | collective-permute-start | bytes 1544 | tf_op jit(solution)/shard_map/ppermute | solution.py:119
  104.1 6.3 %collective-permute-start.6 = (f32[2,64]{1,0:T(2,128)S(1)}, f32[2,64]{1,0:T(2,128)S(1)}, u32[]{:S(2)}, u32[]{:S(2)}) collective-permute-start(f32[2,64]{1,0:T(2,128)S(1)} %collective-permute-done.5), channel_id=1, source_target_pairs={{0,4},{4,8},{8,12},{12,16},{16,20},{20,24},{24,28},{28,0},{1,5},{5... | collective-permute-start | bytes 1544 | tf_op jit(solution)/shard_map/ppermute | solution.py:119
  104.1 12.5 %copy-start.5 = (f32[32,64]{1,0:T(8,128)S(1)}, f32[32,64]{1,0:T(8,128)}, u32[]{:S(2)}) copy-start(f32[32,64]{1,0:T(8,128)} %param.19) | copy-start | bytes 24580
  110.4 6.3 %collective-permute-start.7 = (f32[2,64]{1,0:T(2,128)S(1)}, f32[2,64]{1,0:T(2,128)S(1)}, u32[]{:S(2)}, u32[]{:S(2)}) collective-permute-start(f32[2,64]{1,0:T(2,128)S(1)} %collective-permute-done.6), channel_id=1, source_target_pairs={{0,4},{4,8},{8,12},{12,16},{16,20},{20,24},{24,28},{28,0},{1,5},{5... | collective-permute-start | bytes 1544 | tf_op jit(solution)/shard_map/ppermute | solution.py:119
  116.7 6.3 %collective-permute-start.8 = (f32[2,64]{1,0:T(2,128)S(1)}, f32[2,64]{1,0:T(2,128)S(1)}, u32[]{:S(2)}, u32[]{:S(2)}) collective-permute-start(f32[2,64]{1,0:T(2,128)S(1)} %collective-permute-done.7), channel_id=1, source_target_pairs={{0,4},{4,8},{8,12},{12,16},{16,20},{20,24},{24,28},{28,0},{1,5},{5... | collective-permute-start | bytes 1544 | tf_op jit(solution)/shard_map/ppermute | solution.py:119
  125.0 6.3 %collective-permute-start.9 = (f32[2,64]{1,0:T(2,128)S(1)}, f32[2,64]{1,0:T(2,128)S(1)}, u32[]{:S(2)}, u32[]{:S(2)}) collective-permute-start(f32[2,64]{1,0:T(2,128)S(1)} %slice_reduce_fusion), channel_id=1, source_target_pairs={{0,4},{4,8},{8,12},{12,16},{16,20},{20,24},{24,28},{28,0},{1,5},{5... | collective-permute-start | bytes 1544 | tf_op jit(solution)/shard_map/ppermute | solution.py:119
  131.3 6.3 %collective-permute-start.10 = (f32[2,64]{1,0:T(2,128)S(1)}, f32[2,64]{1,0:T(2,128)S(1)}, u32[]{:S(2)}, u32[]{:S(2)}) collective-permute-start(f32[2,64]{1,0:T(2,128)S(1)} %collective-permute-done.9), channel_id=1, source_target_pairs={{0,4},{4,8},{8,12},{12,16},{16,20},{20,24},{24,28},{28,0},{1,5},{5... | collective-permute-start | bytes 1544 | tf_op jit(solution)/shard_map/ppermute | solution.py:119
  137.6 6.3 %collective-permute-start.11 = (f32[2,64]{1,0:T(2,128)S(1)}, f32[2,64]{1,0:T(2,128)S(1)}, u32[]{:S(2)}, u32[]{:S(2)}) collective-permute-start(f32[2,64]{1,0:T(2,128)S(1)} %collective-permute-done.10), channel_id=1, source_target_pairs={{0,4},{4,8},{8,12},{12,16},{16,20},{20,24},{24,28},{28,0},{1,5},{5... | collective-permute-start | bytes 1544 | tf_op jit(solution)/shard_map/ppermute | solution.py:119
  143.8 6.3 %collective-permute-start.12 = (f32[2,64]{1,0:T(2,128)S(1)}, f32[2,64]{1,0:T(2,128)S(1)}, u32[]{:S(2)}, u32[]{:S(2)}) collective-permute-start(f32[2,64]{1,0:T(2,128)S(1)} %collective-permute-done.11), channel_id=1, source_target_pairs={{0,4},{4,8},{8,12},{12,16},{16,20},{20,24},{24,28},{28,0},{1,5},{5... | collective-permute-start | bytes 1544 | tf_op jit(solution)/shard_map/ppermute | solution.py:119
  150.1 6.3 %collective-permute-start.13 = (f32[2,64]{1,0:T(2,128)S(1)}, f32[2,64]{1,0:T(2,128)S(1)}, u32[]{:S(2)}, u32[]{:S(2)}) collective-permute-start(f32[2,64]{1,0:T(2,128)S(1)} %collective-permute-done.12), channel_id=1, source_target_pairs={{0,4},{4,8},{8,12},{12,16},{16,20},{20,24},{24,28},{28,0},{1,5},{5... | collective-permute-start | bytes 1544 | tf_op jit(solution)/shard_map/ppermute | solution.py:119
  156.4 6.3 %collective-permute-start.14 = (f32[2,64]{1,0:T(2,128)S(1)}, f32[2,64]{1,0:T(2,128)S(1)}, u32[]{:S(2)}, u32[]{:S(2)}) collective-permute-start(f32[2,64]{1,0:T(2,128)S(1)} %collective-permute-done.13), channel_id=1, source_target_pairs={{0,4},{4,8},{8,12},{12,16},{16,20},{20,24},{24,28},{28,0},{1,5},{5... | collective-permute-start | bytes 1544 | tf_op jit(solution)/shard_map/ppermute | solution.py:119
  162.6 6.3 %collective-permute-start.15 = (f32[2,64]{1,0:T(2,128)S(1)}, f32[2,64]{1,0:T(2,128)S(1)}, u32[]{:S(2)}, u32[]{:S(2)}) collective-permute-start(f32[2,64]{1,0:T(2,128)S(1)} %collective-permute-done.14), channel_id=1, source_target_pairs={{0,4},{4,8},{8,12},{12,16},{16,20},{20,24},{24,28},{28,0},{1,5},{5... | collective-permute-start | bytes 1544 | tf_op jit(solution)/shard_map/ppermute | solution.py:119
